TPU v7x, 32 devices: a whole 2x2x4 slice. The times are simulated.
32 devices in a mesh: space: 8 (over z, y), segment: 4 (over x, core).
Axes of the slice: x: 2, y: 2, z: 4, core: 2. Of those that a mesh axis runs over, the one named last changes fastest.
Arguments:
- saved_inputs: bfloat16 [4, 1048576], P('segment', 'space'), may hold values from -5.5 to 5.5
- conv_weights: bfloat16 [4, 221184], P('segment'), may hold values from -0.4375 to 0.4375
- top_gradient: bfloat16 [128, 8, 2, 32], P(None, 'space'), may hold values from -6 to 6
Outputs:
- weight_grads: float32 [4, 221184], P('segment')
All inputs are finite; a program needn't handle non-finite values.
Results may differ from a plain program's by a relative error of at most 0.0023.
Values may be sent and summed in bfloat16 or wider, within the bound.
No kernel may reach another device: no remote copies, remote signals or barrier semaphores. Data moves between devices by JAX's collectives and lax.ppermute only.
A program may use at most 64 MiB of HBM per device.

v0:
```python
import math
import jax
import jax.numpy as jnp
from jax import lax
from jax.sharding import PartitionSpec as P

C0 = 4
C1 = 16
C2 = 32
C3 = 64
C4 = 128
CZ = 4
CY = 8
CX = 128
slope_negative = 0.3
tap_offsets = [
    (tap_z, tap_y, tap_x) for tap_z in range(3) for tap_y in range(3) for tap_x in range(3)
]
parity_terms = [(0, 0, 0), (0, 2, -1), (1, 1, 0)]


def as_sent(x):

    def short(part):
        return part.astype(jnp.bfloat16) if part.dtype == jnp.float32 else part

    return jax.tree.map(short, x)


def with_halo(cells, sides, width):
    for axis, dim in sides:
        count = lax.axis_size(axis)
        ends = count - 1
        head = lax.slice_in_dim(cells, 0, width, axis=dim)
        tail = lax.slice_in_dim(cells, cells.shape[dim] - width, cells.shape[dim], axis=dim)
        cells = jnp.concatenate(
            [
                lax.ppermute(tail, axis, [(i, (i + 1) % count) for i in range(ends)]),
                cells,
                lax.ppermute(head, axis, [((i + 1) % count, i) for i in range(ends)]),
            ],
            axis=dim,
        )
    return cells


def passed_along(block, axis, distance):
    devices = range(lax.axis_size(axis))
    route = [(i - distance, i) for i in devices if i - distance in devices]
    return lax.ppermute(block, axis, route)


def section_table():
    return [
        (C0, C1, 1, CZ, CY, CX),
        (C1, C2, 1, CZ, CY, CX),
        (C2, C3, 2, CZ, CY, CX),
        (C3, C4, 2, CZ // 2, CY // 2, CX // 2),
    ]


def extend_fine(volume):
    return with_halo(as_sent(volume), (("space", 1),), 1).astype(volume.dtype)


def send_back(message):
    return jax.tree.map(
        lambda part, own: part.astype(own.dtype),
        passed_along(as_sent(message), "segment", -1),
        message,
    )


def pad_cross(volume, low_side, high_side):
    return jnp.pad(volume, ((0, 0), (0, 0), (low_side, high_side), (low_side, high_side)))


def fine_weight_grad(act_ext, upstream):
    padded = pad_cross(act_ext, 1, 1)
    out_z, out_y, out_x = (upstream.shape[1], upstream.shape[2], upstream.shape[3])
    results = []
    for tap_z, tap_y, tap_x in tap_offsets:
        window = padded[:, tap_z : tap_z + out_z, tap_y : tap_y + out_y, tap_x : tap_x + out_x]
        results.append(
            jnp.einsum("dzyx,czyx->dc", upstream, window, preferred_element_type=jnp.float32)
        )
    return jnp.stack(results)


def coarse_weight_grad(act_ext, upstream):
    padded = pad_cross(act_ext, 0, 1)
    out_z, out_y, out_x = (upstream.shape[1], upstream.shape[2], upstream.shape[3])
    results = []
    for tap_z, tap_y, tap_x in tap_offsets:
        window = padded[
            :,
            tap_z : tap_z + 2 * out_z : 2,
            tap_y : tap_y + 2 * out_y : 2,
            tap_x : tap_x + 2 * out_x : 2,
        ]
        results.append(
            jnp.einsum("dzyx,czyx->dc", upstream, window, preferred_element_type=jnp.float32)
        )
    return jnp.stack(results)


def fine_input_grad(weights, delta_ext):
    padded = pad_cross(delta_ext, 1, 1)
    size_z, size_y, size_x = (delta_ext.shape[1] - 2, delta_ext.shape[2], delta_ext.shape[3])
    summed = jnp.zeros((weights.shape[2], size_z, size_y, size_x), jnp.float32)
    for position, (tap_z, tap_y, tap_x) in enumerate(tap_offsets):
        window = padded[
            :,
            2 - tap_z : 2 - tap_z + size_z,
            2 - tap_y : 2 - tap_y + size_y,
            2 - tap_x : 2 - tap_x + size_x,
        ]
        summed = summed + jnp.einsum(
            "dc,dzyx->czyx", weights[position], window, preferred_element_type=jnp.float32
        )
    return summed


def coarse_input_grad(weights, delta_ext):
    padded = pad_cross(delta_ext, 1, 0)
    out_z, out_y, out_x = (delta_ext.shape[1] - 1, delta_ext.shape[2], delta_ext.shape[3])
    parity_sums = {}
    for rest_z, tap_z, step_z in parity_terms:
        for rest_y, tap_y, step_y in parity_terms:
            for rest_x, tap_x, step_x in parity_terms:
                window = padded[
                    :,
                    1 + step_z : 1 + step_z + out_z,
                    1 + step_y : 1 + step_y + out_y,
                    1 + step_x : 1 + step_x + out_x,
                ]
                contribution = jnp.einsum(
                    "dc,dzyx->czyx",
                    weights[9 * tap_z + 3 * tap_y + tap_x],
                    window,
                    preferred_element_type=jnp.float32,
                )
                parity = (rest_z, rest_y, rest_x)
                parity_sums[parity] = (
                    parity_sums[parity] + contribution if parity in parity_sums else contribution
                )
    stacked = jnp.stack(
        [
            jnp.stack(
                [
                    jnp.stack([parity_sums[rest_z, rest_y, rest_x] for rest_x in (0, 1)])
                    for rest_y in (0, 1)
                ]
            )
            for rest_z in (0, 1)
        ]
    )
    channels = weights.shape[2]
    return jnp.transpose(stacked, (3, 4, 0, 5, 1, 6, 2)).reshape(
        channels, 2 * out_z, 2 * out_y, 2 * out_x
    )


def weight_term(act_ext, upstream, stride_size, scale_factor):
    if stride_size == 1:
        return fine_weight_grad(act_ext, upstream) * scale_factor
    return coarse_weight_grad(act_ext, upstream) * scale_factor


def message_term(weights, delta_ext, activation, stride_size):
    if stride_size == 1:
        backward = fine_input_grad(weights, delta_ext)
    else:
        backward = coarse_input_grad(weights, delta_ext)
    return (backward * jnp.where(activation > 0, 1.0, slope_negative)).astype(jnp.bfloat16)


def shards(saved_inputs, conv_weights, top_gradient):
    segment_index = lax.axis_index("segment")
    space_count = lax.axis_size("space")
    own_row = saved_inputs[0]
    own_weights = conv_weights[0]
    weight_room = conv_weights.shape[1]
    upstream = top_gradient
    collected = jnp.zeros((weight_room,), jnp.float32)
    for section in (3, 2, 1, 0):
        chan_in, chan_out, stride_size, depth_cells, height, breadth = section_table()[section]
        activation = own_row[: chan_in * depth_cells * height * breadth].reshape(
            chan_in, depth_cells, height, breadth
        )
        weights = own_weights[: 27 * chan_out * chan_in].reshape(27, chan_out, chan_in)
        active = segment_index == section
        scale_factor = 1.0 / math.sqrt(
            space_count * upstream.shape[1] * upstream.shape[2] * upstream.shape[3]
        )
        if stride_size == 1:
            if section > 0:
                joined = extend_fine(jnp.concatenate([activation, upstream], 0))
                act_ext = joined[:chan_in]
                delta_ext = joined[chan_in:]
            else:
                act_ext = extend_fine(activation)
                delta_ext = upstream
        else:
            upper_plane = passed_along(activation[:, :1], "space", -1)
            lower_plane = passed_along(as_sent(upstream[:, -1:]), "space", 1)
            act_ext = jnp.concatenate([activation, upper_plane], 1)
            delta_ext = jnp.concatenate([lower_plane, upstream], 1)
        grad_shape = (27, chan_out, chan_in)
        message_shape = activation.shape

        def weight_branch(act_ext, upstream, stride_size=stride_size, scale_factor=scale_factor):
            return weight_term(act_ext, upstream, stride_size, scale_factor)

        def weight_skip(act_ext, upstream, grad_shape=grad_shape):
            return jnp.zeros(grad_shape, jnp.float32)

        def both_branch(
            weights,
            delta_ext,
            activation,
            act_ext,
            upstream,
            stride_size=stride_size,
            scale_factor=scale_factor,
        ):
            return (
                weight_term(act_ext, upstream, stride_size, scale_factor),
                message_term(weights, delta_ext, activation, stride_size),
            )

        def both_skip(
            weights,
            delta_ext,
            activation,
            act_ext,
            upstream,
            grad_shape=grad_shape,
            message_shape=message_shape,
        ):
            return (jnp.zeros(grad_shape, jnp.float32), jnp.zeros(message_shape, jnp.bfloat16))

        if section > 0:
            local_grad, message = lax.cond(
                active, both_branch, both_skip, weights, delta_ext, activation, act_ext, upstream
            )
            passed = send_back(message)
        else:
            local_grad = lax.cond(active, weight_branch, weight_skip, act_ext, upstream)
        local_grad = lax.psum(local_grad, "space")
        flat_grad = local_grad.reshape(-1)
        collected = jnp.where(
            active, jnp.pad(flat_grad, (0, weight_room - flat_grad.shape[0])), collected
        )
        if section > 0:
            upstream = passed
    return collected[None]


def solution(mesh):
    return jax.shard_map(
        shards,
        mesh=mesh,
        in_specs=(P("segment", "space"), P("segment", None), P(None, "space", None, None)),
        out_specs=P("segment", None),
        check_vma=False,
    )
```

profile of v0, /device:TPU:0, one launch (start us, length us, event | category | flops | bytes accessed | tf_op | source)
XLA Modules:
  0.0 222.7 jit_solution(12516245438822264180)
XLA Ops:
  6.5 4.9 %collective-permute-start.4 = (bf16[128,1,2,32]{0,3,2,1:T(8,128)(2,1)}, bf16[128,1,2,32]{0,3,2,1:T(8,128)(2,1)S(1)}, u32[]{:S(2)}, u32[]{:S(2)}) collective-permute-start(bf16[128,1,2,32]{0,3,2,1:T(8,128)(2,1)} %param.13), channel_id=1, source_target_pairs={{0,4},{4,8},{8,12},{12,16},{16,20},{20,24},{24,28},{1,5},{5,9},{9,... | collective-permute-start | bytes 49160 | tf_op jit(solution)/shard_map/ppermute | solution.py:50
  11.4 1.3 slice_reduce_fusion.82
  12.8 1.3 collective-permute-start.3
  14.1 0.7 pad_maximum_fusion.5
  14.9 4.1 %collective-permute-done.3 = bf16[64,1,4,64]{3,2,1,0:T(4,128)(2,1)S(1)} collective-permute-done((bf16[64,1,4,64]{3,2,1,0:T(4,128)(2,1)S(1)}, bf16[64,1,4,64]{3,2,1,0:T(4,128)(2,1)S(1)}, u32[]{:S(2)}, u32[]{:S(2)}) %collective-permute-start.3) | collective-permute-done | bytes 32800 | tf_op jit(solution)/shard_map/ppermute | solution.py:50
  19.2 0.8 conditional.4
  19.3 0.7 broadcast.33
  19.9 0.9 copy-done.1
  20.9 1.0 copy.205
  21.9 1.3 collective-permute-start.5
  23.2 1.6 reduce.83
  24.8 1.3 collective-permute-start.2
  26.1 5.0 %collective-permute-start.6 = (bf16[64,1,4,64]{3,0,2,1:T(8,128)(2,1)S(1)}, bf16[64,1,4,64]{3,0,2,1:T(8,128)(2,1)S(1)}, u32[]{:S(2)}, u32[]{:S(2)}) collective-permute-start(bf16[64,1,4,64]{3,0,2,1:T(8,128)(2,1)S(1)} %copy.463), channel_id=1, source_target_pairs={{0,4},{4,8},{8,12},{12,16},{16,20},{20,24},{24,28},{1,5},{5,9},{9,... | collective-permute-start | bytes 98312 | tf_op jit(solution)/shard_map/ppermute | solution.py:50
  31.1 0.6 collective-permute-done.2
  31.7 0.8 pad_maximum_fusion.1
  32.5 1.4 collective-permute-done.6
  33.9 2.1 conditional.5
  33.9 1.2 broadcast.41
  35.2 0.8 broadcast.40
  36.0 1.6 copy.210
  37.6 1.3 collective-permute-start.7
  38.9 1.7 slice_reduce_fusion.81
  40.6 1.3 copy.217
  41.9 0.9 reshape.416
  43.0 4.4 %collective-permute-start.8 = (bf16[48,1,8,128]{3,0,1,2:T(8,128)(2,1)S(1)}, bf16[48,1,8,128]{3,0,1,2:T(8,128)(2,1)S(1)}, u32[]{:S(2)}, u32[]{:S(2)}) collective-permute-start(bf16[48,1,8,128]{3,0,1,2:T(8,128)(2,1)S(1)} %get-tuple-element.206), channel_id=1, source_target_pairs={{0,4},{4,8},{8,12},{12,16},{16,20},{20,24},{24,28},{1,5},{5,9},{9,... | collective-permute-start | bytes 294920 | tf_op jit(solution)/shard_map/ppermute | solution.py:38
  47.4 1.3 collective-permute-start.9
  48.7 1.0 slice_reduce_fusion.83
  49.8 5.5 %collective-permute-done.9 = bf16[48,1,8,128]{3,0,1,2:T(8,128)(2,1)S(1)} collective-permute-done((bf16[48,1,8,128]{3,0,1,2:T(8,128)(2,1)S(1)}, bf16[48,1,8,128]{3,0,1,2:T(8,128)(2,1)S(1)}, u32[]{:S(2)}, u32[]{:S(2)}) %collective-permute-start.9) | collective-permute-done | bytes 98336 | tf_op jit(solution)/shard_map/ppermute | solution.py:40
  55.4 0.3 conditional.6
  55.7 1.3 collective-permute-start.10
  57.0 4.8 %collective-permute-start = (bf16[4,1,8,128]{3,2,1,0:T(8,128)(2,1)S(1)}, bf16[4,1,8,128]{3,2,1,0:T(8,128)(2,1)S(1)}, u32[]{:S(2)}, u32[]{:S(2)}) collective-permute-start(bf16[4,1,8,128]{3,2,1,0:T(8,128)(2,1)S(1)} %get-tuple-element.208), channel_id=1, source_target_pairs={{0,4},{4,8},{8,12},{12,16},{16,20},{20,24},{24,28},{1,5},{5,9},{9,... | collective-permute-start | bytes 24584 | tf_op jit(solution)/shard_map/ppermute | solution.py:38
  61.8 1.3 collective-permute-start.1
  63.2 4.2 %collective-permute-done.1 = bf16[4,1,8,128]{3,2,1,0:T(8,128)(2,1)S(1)} collective-permute-done((bf16[4,1,8,128]{3,2,1,0:T(8,128)(2,1)S(1)}, bf16[4,1,8,128]{3,2,1,0:T(8,128)(2,1)S(1)}, u32[]{:S(2)}, u32[]{:S(2)}) %collective-permute-start.1) | collective-permute-done | bytes 8224 | tf_op jit(solution)/shard_map/ppermute | solution.py:40
  67.8 98.1 %collective-permute-done.10 = bf16[16,4,8,128]{3,0,1,2:T(8,128)(2,1)S(1)} collective-permute-done((bf16[16,4,8,128]{3,0,1,2:T(8,128)(2,1)S(1)}, bf16[16,4,8,128]{3,0,1,2:T(8,128)(2,1)S(1)}, u32[]{:S(2)}, u32[]{:S(2)}) %collective-permute-start.10) | collective-permute-done | bytes 131104 | tf_op jit(solution)/shard_map/ppermute | solution.py:50
  165.8 6.0 %conditional.7 = (f32[27,16,4]{1,2,0:T(4,128)S(1)}) conditional(s32[]{:T(128)} %convert_element_type.41, () %tuple.35, (bf16[4,6,8,128]{3,2,1,0:T(8,128)(2,1)S(1)}, bf16[16,4,8,128]{3,0,1,2:T(8,128)(2,1)S(1)}) %tuple.42), branch_computations={%region_6.7_spmd, %region_7.8_spmd} | conditional | flops 14157503 | bytes 4984328 | solution.py:249
  166.5 0.2 fusion.23
  166.9 0.2 fusion.21
  167.1 0.2 fusion.20
  168.5 0.2 fusion.14
  168.9 0.2 fusion.12
  169.6 0.2 fusion.9
  170.5 0.2 fusion.5
  170.9 0.2 fusion.3
  172.2 37.4 %all-reduce.10 = (f32[13824]{0:T(1024)S(1)}, f32[1728]{0:T(1024)S(1)}) all-reduce(f32[13824]{0:T(1024)S(1)} %reshape.415, f32[1728]{0:T(1024)S(1)} %reshape.414), channel_id=1, replica_groups=mesh['space'=8,'segment'=4] {'space'}, use_global_device_ids=true, to_apply=%region_9.10 | all-reduce | flops 15552 | bytes 124416 | tf_op jit(solution)/shard_map/psum | solution.py:250
  209.6 4.2 %all-reduce.14.cloned.1.call-done = (f32[27,128,64]{1,2,0:T(8,128)}, f32[55296]{0:T(1024)}) async-done(((f32[27,128,64]{1,2,0:T(8,128)}, f32[55296]{0:T(1024)}), (f32[27,128,64]{1,2,0:T(8,128)}, f32[55296]{0:T(1024)})) %all-reduce.14.cloned.1.call-update) | async-done | bytes 1105936 | tf_op jit(solution)/shard_map/psum | solution.py:250
  213.9 0.5 copy.218
  214.4 0.3 select_n.46
  214.8 1.0 select_select_fusion
  (55 shorter events, 5.7 us)
Async XLA Ops:
  6.5 207.3 %all-reduce.14.cloned.1.call-start = ((), (), s32[]{:S(2)}) async-start(), calls=%async_computation | async-start | bytes 2211840 | tf_op jit(solution)/shard_map/psum | solution.py:250
  6.5 7.6 %collective-permute-start.4 = (bf16[128,1,2,32]{0,3,2,1:T(8,128)(2,1)}, bf16[128,1,2,32]{0,3,2,1:T(8,128)(2,1)S(1)}, u32[]{:S(2)}, u32[]{:S(2)}) collective-permute-start(bf16[128,1,2,32]{0,3,2,1:T(8,128)(2,1)} %param.13), channel_id=1, source_target_pairs={{0,4},{4,8},{8,12},{12,16},{16,20},{20,24},{24,28},{1,5},{5,9},{9,... | collective-permute-start | bytes 49160 | tf_op jit(solution)/shard_map/ppermute | solution.py:50
  12.8 6.2 %collective-permute-start.3 = (bf16[64,1,4,64]{3,2,1,0:T(4,128)(2,1)S(1)}, bf16[64,1,4,64]{3,2,1,0:T(4,128)(2,1)S(1)}, u32[]{:S(2)}, u32[]{:S(2)}) collective-permute-start(bf16[64,1,4,64]{3,2,1,0:T(4,128)(2,1)S(1)} %slice.982), channel_id=1, source_target_pairs={{4,0},{8,4},{12,8},{16,12},{20,16},{24,20},{28,24},{5,1},{9,5},{13... | collective-permute-start | bytes 98312 | tf_op jit(solution)/shard_map/ppermute | solution.py:50
  19.2 4.0 %copy-start.2 = (bf16[1,131072]{1,0:T(2,128)(2,1)S(1)}, bf16[1,131072]{1,0:T(2,128)(2,1)}, u32[]{:S(2)}) copy-start(bf16[1,131072]{1,0:T(2,128)(2,1)} %param.11) | copy-start | bytes 786436
  19.9 0.9 copy-start.1
  21.9 4.2 %collective-permute-start.5 = (bf16[64,2,4,64]{3,0,1,2:T(8,128)(2,1)S(1)}, bf16[64,2,4,64]{3,0,1,2:T(8,128)(2,1)S(1)}, u32[]{:S(2)}, u32[]{:S(2)}) collective-permute-start(bf16[64,2,4,64]{3,0,1,2:T(8,128)(2,1)S(1)} %copy.205), channel_id=1, source_target_pairs={{1,0},{2,1},{3,2},{5,4},{6,5},{7,6},{9,8},{10,9},{11,10},{13,12},{... | collective-permute-start | bytes 196616 | tf_op jit(solution)/shard_map/ppermute | solution.py:50
  24.8 6.9 %collective-permute-start.2 = (bf16[32,1,8,128]{3,2,1,0:T(8,128)(2,1)S(1)}, bf16[32,1,8,128]{3,2,1,0:T(8,128)(2,1)S(1)}, u32[]{:S(2)}, u32[]{:S(2)}) collective-permute-start(bf16[32,1,8,128]{3,2,1,0:T(8,128)(2,1)S(1)} %slice.981), channel_id=1, source_target_pairs={{4,0},{8,4},{12,8},{16,12},{20,16},{24,20},{28,24},{5,1},{9,5},{13... | collective-permute-start | bytes 196616 | tf_op jit(solution)/shard_map/ppermute | solution.py:50
  26.1 7.7 %collective-permute-start.6 = (bf16[64,1,4,64]{3,0,2,1:T(8,128)(2,1)S(1)}, bf16[64,1,4,64]{3,0,2,1:T(8,128)(2,1)S(1)}, u32[]{:S(2)}, u32[]{:S(2)}) collective-permute-start(bf16[64,1,4,64]{3,0,2,1:T(8,128)(2,1)S(1)} %copy.463), channel_id=1, source_target_pairs={{0,4},{4,8},{8,12},{12,16},{16,20},{20,24},{24,28},{1,5},{5,9},{9,... | collective-permute-start | bytes 98312 | tf_op jit(solution)/shard_map/ppermute | solution.py:50
  37.6 5.4 %collective-permute-start.7 = (bf16[32,4,8,128]{3,0,1,2:T(8,128)(2,1)S(1)}, bf16[32,4,8,128]{3,0,1,2:T(8,128)(2,1)S(1)}, u32[]{:S(2)}, u32[]{:S(2)}) collective-permute-start(bf16[32,4,8,128]{3,0,1,2:T(8,128)(2,1)S(1)} %copy.210), channel_id=1, source_target_pairs={{1,0},{2,1},{3,2},{5,4},{6,5},{7,6},{9,8},{10,9},{11,10},{13,12},{... | collective-permute-start | bytes 786440 | tf_op jit(solution)/shard_map/ppermute | solution.py:50
  43.0 6.7 %collective-permute-start.8 = (bf16[48,1,8,128]{3,0,1,2:T(8,128)(2,1)S(1)}, bf16[48,1,8,128]{3,0,1,2:T(8,128)(2,1)S(1)}, u32[]{:S(2)}, u32[]{:S(2)}) collective-permute-start(bf16[48,1,8,128]{3,0,1,2:T(8,128)(2,1)S(1)} %get-tuple-element.206), channel_id=1, source_target_pairs={{0,4},{4,8},{8,12},{12,16},{16,20},{20,24},{24,28},{1,5},{5,9},{9,... | collective-permute-start | bytes 294920 | tf_op jit(solution)/shard_map/ppermute | solution.py:38
  47.4 7.9 %collective-permute-start.9 = (bf16[48,1,8,128]{3,0,1,2:T(8,128)(2,1)S(1)}, bf16[48,1,8,128]{3,0,1,2:T(8,128)(2,1)S(1)}, u32[]{:S(2)}, u32[]{:S(2)}) collective-permute-start(bf16[48,1,8,128]{3,0,1,2:T(8,128)(2,1)S(1)} %get-tuple-element.207), channel_id=1, source_target_pairs={{4,0},{8,4},{12,8},{16,12},{20,16},{24,20},{28,24},{5,1},{9,5},{13... | collective-permute-start | bytes 294920 | tf_op jit(solution)/shard_map/ppermute | solution.py:40
  55.7 110.1 %collective-permute-start.10 = (bf16[16,4,8,128]{3,0,1,2:T(8,128)(2,1)S(1)}, bf16[16,4,8,128]{3,0,1,2:T(8,128)(2,1)S(1)}, u32[]{:S(2)}, u32[]{:S(2)}) collective-permute-start(bf16[16,4,8,128]{3,0,1,2:T(8,128)(2,1)S(1)} %copy.213), channel_id=1, source_target_pairs={{1,0},{2,1},{3,2},{5,4},{6,5},{7,6},{9,8},{10,9},{11,10},{13,12},{... | collective-permute-start | bytes 393224 | tf_op jit(solution)/shard_map/ppermute | solution.py:50
  57.0 6.2 %collective-permute-start = (bf16[4,1,8,128]{3,2,1,0:T(8,128)(2,1)S(1)}, bf16[4,1,8,128]{3,2,1,0:T(8,128)(2,1)S(1)}, u32[]{:S(2)}, u32[]{:S(2)}) collective-permute-start(bf16[4,1,8,128]{3,2,1,0:T(8,128)(2,1)S(1)} %get-tuple-element.208), channel_id=1, source_target_pairs={{0,4},{4,8},{8,12},{12,16},{16,20},{20,24},{24,28},{1,5},{5,9},{9,... | collective-permute-start | bytes 24584 | tf_op jit(solution)/shard_map/ppermute | solution.py:38
  61.8 5.5 %collective-permute-start.1 = (bf16[4,1,8,128]{3,2,1,0:T(8,128)(2,1)S(1)}, bf16[4,1,8,128]{3,2,1,0:T(8,128)(2,1)S(1)}, u32[]{:S(2)}, u32[]{:S(2)}) collective-permute-start(bf16[4,1,8,128]{3,2,1,0:T(8,128)(2,1)S(1)} %get-tuple-element.209), channel_id=1, source_target_pairs={{4,0},{8,4},{12,8},{16,12},{20,16},{24,20},{28,24},{5,1},{9,5},{13... | collective-permute-start | bytes 24584 | tf_op jit(solution)/shard_map/ppermute | solution.py:40
  213.9 0.9 copy-start.5
Sparse Core Ops, SparseCore 0:
  43.0 170.7 all-reduce.13
where the time goes:
time: 224 us; the launch traced here: 223 us
  waiting for transfers between devices  118 us (53%)
  blocking collectives  37.4 us (17%)
  starting transfers between devices  28.1 us (13%)
  local copies, waits for them, and re-layouts  14.6 us (7%)
  between operations  13.7 us (6%)
  matrix products  5.93 us (3%)
  other arithmetic  4.47 us (2%)
    ppermute x7, waiting for transfers between devices, passed_along(): return lax.ppermute(block, axis, route)  104 us
    psum x1, blocking collectives, shards(): local_grad = lax.psum(local_grad, 'space')  37.4 us
    ppermute x7, starting transfers between devices, passed_along(): return lax.ppermute(block, axis, route)  16.3 us
    ppermute x2, waiting for transfers between devices, with_halo(): lax.ppermute(head, axis, [((i + 1) % count, i) for i in range(ends)])  9.74 us
    ppermute x2, starting transfers between devices, with_halo(): lax.ppermute(tail, axis, [(i, (i + 1) % count) for i in range(ends)])  9.21 us
    dot_general x27, matrix products, fine_weight_grad(): jnp.einsum('dzyx,czyx->dc', upstream, window, preferred_element_type=jnp....  5.93 us
  transfers between devices with their start and end apart: 12, of which 7 were waited for; matrix products, arithmetic and copies ran while one was open for 7% of the time, Pallas kernels for 0%

commit v1 on v0

--- a/solution.py
+++ b/solution.py
@@ -247,7 +247,7 @@
             passed = send_back(message)
         else:
             local_grad = lax.cond(active, weight_branch, weight_skip, act_ext, upstream)
-        local_grad = lax.psum(local_grad, "space")
+        local_grad = jnp.sum(lax.all_gather(local_grad, "space"), axis=0)
         flat_grad = local_grad.reshape(-1)
         collected = jnp.where(
             active, jnp.pad(flat_grad, (0, weight_room - flat_grad.shape[0])), collected

time: 224 us -> 346 us (1.54)
  waiting for transfers between devices: 118 us -> 199 us
  blocking collectives: 37.4 us -> 72 us
  other arithmetic: 4.47 us -> 10.3 us
    all_gather x0 -> x2, waiting for transfers between devices: none -> 111 us  [shards(): local_grad = jnp.sum(lax.all_gather(local_grad, 'space'), axis=0)]
    all_gather x0 -> x2, blocking collectives: none -> 72 us  [shards(): local_grad = jnp.sum(lax.all_gather(local_grad, 'space'), axis=0)]
    psum x1 -> x0, blocking collectives: 37.4 us -> none  [shards(): local_grad = lax.psum(local_grad, 'space')]
    ppermute x7, waiting for transfers between devices: 104 us -> 85.8 us  [passed_along(): return lax.ppermute(block, axis, route)]
    ppermute x2, waiting for transfers between devices: 9.74 us -> 0.61 us  [with_halo(): lax.ppermute(head, axis, [((i + 1) % count, i) for i in range(ends)])]
    reduce_sum x0 -> x4, other arithmetic: none -> 6.57 us  [shards(): local_grad = jnp.sum(lax.all_gather(local_grad, 'space'), axis=0)]
    psum x1 -> x0, waiting for transfers between devices: 4.18 us -> none  [shards(): local_grad = lax.psum(local_grad, 'space')]
  transfers between devices with their start and end apart: 12 -> 13, of which waited for: 7 -> 8; matrix products, arithmetic and copies ran while one was open for 7% -> 5% of each run, Pallas kernels for 0% -> 0%
where the time goes in v1:
time: 346 us; the launch traced here: 344 us
  waiting for transfers between devices  199 us (58%)
  blocking collectives  72 us (21%)
  starting transfers between devices  29.8 us (9%)
  between operations  13.8 us (4%)
  local copies, waits for them, and re-layouts  12.5 us (4%)
  other arithmetic  10.3 us (3%)
  matrix products  5.93 us (2%)
    all_gather x2, waiting for transfers between devices, shards(): local_grad = jnp.sum(lax.all_gather(local_grad, 'space'), axis=0)  111 us
    ppermute x7, waiting for transfers between devices, passed_along(): return lax.ppermute(block, axis, route)  85.8 us
    all_gather x2, blocking collectives, shards(): local_grad = jnp.sum(lax.all_gather(local_grad, 'space'), axis=0)  72 us
    ppermute x7, starting transfers between devices, passed_along(): return lax.ppermute(block, axis, route)  16.3 us
    ppermute x2, starting transfers between devices, with_halo(): lax.ppermute(tail, axis, [(i, (i + 1) % count) for i in range(ends)])  10.9 us
  transfers between devices with their start and end apart: 13, of which 8 were waited for; matrix products, arithmetic and copies ran while one was open for 5% of the time, Pallas kernels for 0%

profile of v1, /device:TPU:0, one launch (start us, length us, event | category | flops | bytes accessed | tf_op | source)
XLA Modules:
  0.0 344.0 jit_solution(8148631303813910024)
XLA Ops:
  6.5 4.9 %collective-permute-start.4 = (bf16[128,1,2,32]{0,3,2,1:T(8,128)(2,1)}, bf16[128,1,2,32]{0,3,2,1:T(8,128)(2,1)S(1)}, u32[]{:S(2)}, u32[]{:S(2)}) collective-permute-start(bf16[128,1,2,32]{0,3,2,1:T(8,128)(2,1)} %param.13), channel_id=1, source_target_pairs={{0,4},{4,8},{8,12},{12,16},{16,20},{20,24},{24,28},{1,5},{5,9},{9,... | collective-permute-start | bytes 49160 | tf_op jit(solution)/shard_map/ppermute | solution.py:50
  11.4 1.3 slice_reduce_fusion.82
  12.8 1.3 collective-permute-start.3
  14.1 0.7 pad_maximum_fusion.5
  14.9 4.1 %collective-permute-done.3 = bf16[64,1,4,64]{3,2,1,0:T(4,128)(2,1)S(1)} collective-permute-done((bf16[64,1,4,64]{3,2,1,0:T(4,128)(2,1)S(1)}, bf16[64,1,4,64]{3,2,1,0:T(4,128)(2,1)S(1)}, u32[]{:S(2)}, u32[]{:S(2)}) %collective-permute-start.3) | collective-permute-done | bytes 32800 | tf_op jit(solution)/shard_map/ppermute | solution.py:50
  19.2 0.8 conditional.4
  19.3 0.7 broadcast.33
  19.9 0.9 copy-done.1
  20.9 1.0 copy.300
  21.9 1.3 collective-permute-start.5
  23.2 1.6 reduce.83
  24.8 1.3 collective-permute-start.2
  26.1 5.0 %collective-permute-start.6 = (bf16[64,1,4,64]{3,0,2,1:T(8,128)(2,1)S(1)}, bf16[64,1,4,64]{3,0,2,1:T(8,128)(2,1)S(1)}, u32[]{:S(2)}, u32[]{:S(2)}) collective-permute-start(bf16[64,1,4,64]{3,0,2,1:T(8,128)(2,1)S(1)} %copy.558), channel_id=1, source_target_pairs={{0,4},{4,8},{8,12},{12,16},{16,20},{20,24},{24,28},{1,5},{5,9},{9,... | collective-permute-start | bytes 98312 | tf_op jit(solution)/shard_map/ppermute | solution.py:50
  31.1 0.6 collective-permute-done.2
  31.7 2.1 collective-permute-done.6
  33.9 2.1 conditional.5
  33.9 0.8 broadcast.40
  34.7 1.2 broadcast.41
  36.0 0.7 all-gather.9.cloned.1.call-update
  36.7 1.0 slice_reduce_fusion.83
  37.8 1.3 collective-permute-start.1
  39.1 5.0 %collective-permute-start = (bf16[4,1,8,128]{3,2,1,0:T(8,128)(2,1)S(1)}, bf16[4,1,8,128]{3,2,1,0:T(8,128)(2,1)S(1)}, u32[]{:S(2)}, u32[]{:S(2)}) collective-permute-start(bf16[4,1,8,128]{3,2,1,0:T(8,128)(2,1)S(1)} %get-tuple-element.220), channel_id=1, source_target_pairs={{0,4},{4,8},{8,12},{12,16},{16,20},{20,24},{24,28},{1,5},{5,9},{9,... | collective-permute-start | bytes 24584 | tf_op jit(solution)/shard_map/ppermute | solution.py:38
  44.1 1.6 copy.305
  45.7 1.3 collective-permute-start.7
  47.0 0.7 slice_reduce_fusion.81
  47.8 1.3 collective-permute-done.7
  49.2 1.3 collective-permute-start.9
  50.5 5.9 %collective-permute-start.8 = (bf16[48,1,8,128]{3,0,1,2:T(8,128)(2,1)S(1)}, bf16[48,1,8,128]{3,0,1,2:T(8,128)(2,1)S(1)}, u32[]{:S(2)}, u32[]{:S(2)}) collective-permute-start(bf16[48,1,8,128]{3,0,1,2:T(8,128)(2,1)S(1)} %get-tuple-element.218), channel_id=1, source_target_pairs={{0,4},{4,8},{8,12},{12,16},{16,20},{20,24},{24,28},{1,5},{5,9},{9,... | collective-permute-start | bytes 294920 | tf_op jit(solution)/shard_map/ppermute | solution.py:38
  56.5 0.6 collective-permute-done.9
  57.1 1.5 collective-permute-done.8
  58.7 1.0 conditional.6
  58.7 0.7 broadcast.48
  59.7 1.3 collective-permute-start.10
  61.0 37.0 %all-gather.1 = f32[216,32,16]{1,2,0:T(8,128)S(1)} all-gather(f32[27,32,16]{1,2,0:T(8,128)} %get-tuple-element.73), channel_id=3, replica_groups=mesh['space'=8,'segment'=4] {'space'}, dimensions={0}, use_global_device_ids=true | all-gather | bytes 497664 | tf_op jit(solution)/shard_map/all_gather | solution.py:250
  98.5 77.6 %collective-permute-done.10 = bf16[16,4,8,128]{3,0,1,2:T(8,128)(2,1)S(1)} collective-permute-done((bf16[16,4,8,128]{3,0,1,2:T(8,128)(2,1)S(1)}, bf16[16,4,8,128]{3,0,1,2:T(8,128)(2,1)S(1)}, u32[]{:S(2)}, u32[]{:S(2)}) %collective-permute-start.10) | collective-permute-done | bytes 131104 | tf_op jit(solution)/shard_map/ppermute | solution.py:50
  176.1 6.0 %conditional.7 = (f32[27,16,4]{1,2,0:T(4,128)S(1)}) conditional(s32[]{:T(128)} %convert_element_type.41, () %tuple.35, (bf16[4,6,8,128]{3,2,1,0:T(8,128)(2,1)S(1)}, bf16[16,4,8,128]{3,0,1,2:T(8,128)(2,1)S(1)}) %tuple.42), branch_computations={%region_6.7_spmd, %region_7.8_spmd} | conditional | flops 14157503 | bytes 4984328 | solution.py:249
  176.8 0.2 fusion.23
  178.7 0.2 fusion.14
  180.7 0.2 fusion.5
  181.2 0.2 fusion.3
  182.1 35.0 %all-gather = f32[216,16,4]{1,2,0:T(4,128)S(1)} all-gather(f32[27,16,4]{1,2,0:T(4,128)S(1)} %get-tuple-element.234), channel_id=2, replica_groups=mesh['space'=8,'segment'=4] {'space'}, dimensions={0}, use_global_device_ids=true | all-gather | bytes 62208 | tf_op jit(solution)/shard_map/all_gather | solution.py:250
  217.7 2.5 reduce_sum.38
  220.2 0.3 copy.312
  220.7 110.6 %all-gather.9.cloned.1.call-done = f32[216,128,64]{1,2,0:T(8,128)} async-done(((f32[27,128,64]{1,2,0:T(8,128)}), f32[216,128,64]{1,2,0:T(8,128)}) %all-gather.9.cloned.1.call-update) | async-done | bytes 7077904 | tf_op jit(solution)/shard_map/all_gather | solution.py:250
  331.3 3.8 %reduce_sum.39 = f32[27,128,64]{1,2,0:T(8,128)S(1)} reduce(f32[8,27,128,64]{2,3,1,0:T(8,128)} %bitcast.1839, f32[]{:T(128)} %constant.64.clone.1), dimensions={0}, to_apply=%region_11.12 | reduce | flops 1548288 | bytes 7962628 | tf_op jit(solution)/shard_map/reduce_sum | solution.py:250
  335.2 0.5 copy.313
  335.8 0.3 select_n.46
  336.1 1.0 select_select_fusion
  (63 shorter events, 7.1 us)
Async XLA Ops:
  6.5 211.1 %all-gather.7.cloned.1.call-start = ((), (), s32[]{:S(2)}) async-start(), calls=%async_computation | async-start | bytes 3981312 | tf_op jit(solution)/shard_map/all_gather | solution.py:250
  6.5 7.6 %collective-permute-start.4 = (bf16[128,1,2,32]{0,3,2,1:T(8,128)(2,1)}, bf16[128,1,2,32]{0,3,2,1:T(8,128)(2,1)S(1)}, u32[]{:S(2)}, u32[]{:S(2)}) collective-permute-start(bf16[128,1,2,32]{0,3,2,1:T(8,128)(2,1)} %param.13), channel_id=1, source_target_pairs={{0,4},{4,8},{8,12},{12,16},{16,20},{20,24},{24,28},{1,5},{5,9},{9,... | collective-permute-start | bytes 49160 | tf_op jit(solution)/shard_map/ppermute | solution.py:50
  12.8 6.2 %collective-permute-start.3 = (bf16[64,1,4,64]{3,2,1,0:T(4,128)(2,1)S(1)}, bf16[64,1,4,64]{3,2,1,0:T(4,128)(2,1)S(1)}, u32[]{:S(2)}, u32[]{:S(2)}) collective-permute-start(bf16[64,1,4,64]{3,2,1,0:T(4,128)(2,1)S(1)} %slice.982), channel_id=1, source_target_pairs={{4,0},{8,4},{12,8},{16,12},{20,16},{24,20},{28,24},{5,1},{9,5},{13... | collective-permute-start | bytes 98312 | tf_op jit(solution)/shard_map/ppermute | solution.py:50
  19.2 4.0 %copy-start.2 = (bf16[1,131072]{1,0:T(2,128)(2,1)S(1)}, bf16[1,131072]{1,0:T(2,128)(2,1)}, u32[]{:S(2)}) copy-start(bf16[1,131072]{1,0:T(2,128)(2,1)} %param.11) | copy-start | bytes 786436
  19.9 0.9 copy-start.1
  21.9 4.2 %collective-permute-start.5 = (bf16[64,2,4,64]{3,0,1,2:T(8,128)(2,1)S(1)}, bf16[64,2,4,64]{3,0,1,2:T(8,128)(2,1)S(1)}, u32[]{:S(2)}, u32[]{:S(2)}) collective-permute-start(bf16[64,2,4,64]{3,0,1,2:T(8,128)(2,1)S(1)} %copy.300), channel_id=1, source_target_pairs={{1,0},{2,1},{3,2},{5,4},{6,5},{7,6},{9,8},{10,9},{11,10},{13,12},{... | collective-permute-start | bytes 196616 | tf_op jit(solution)/shard_map/ppermute | solution.py:50
  24.8 6.9 %collective-permute-start.2 = (bf16[32,1,8,128]{3,2,1,0:T(8,128)(2,1)S(1)}, bf16[32,1,8,128]{3,2,1,0:T(8,128)(2,1)S(1)}, u32[]{:S(2)}, u32[]{:S(2)}) collective-permute-start(bf16[32,1,8,128]{3,2,1,0:T(8,128)(2,1)S(1)} %slice.981), channel_id=1, source_target_pairs={{4,0},{8,4},{12,8},{16,12},{20,16},{24,20},{28,24},{5,1},{9,5},{13... | collective-permute-start | bytes 196616 | tf_op jit(solution)/shard_map/ppermute | solution.py:50
  26.1 7.7 %collective-permute-start.6 = (bf16[64,1,4,64]{3,0,2,1:T(8,128)(2,1)S(1)}, bf16[64,1,4,64]{3,0,2,1:T(8,128)(2,1)S(1)}, u32[]{:S(2)}, u32[]{:S(2)}) collective-permute-start(bf16[64,1,4,64]{3,0,2,1:T(8,128)(2,1)S(1)} %copy.558), channel_id=1, source_target_pairs={{0,4},{4,8},{8,12},{12,16},{16,20},{20,24},{24,28},{1,5},{5,9},{9,... | collective-permute-start | bytes 98312 | tf_op jit(solution)/shard_map/ppermute | solution.py:50
  36.0 11.0 %copy-start.3 = (bf16[1,131072]{1,0:T(2,128)(2,1)S(1)}, bf16[1,131072]{1,0:T(2,128)(2,1)}, u32[]{:S(2)}) copy-start(bf16[1,131072]{1,0:T(2,128)(2,1)} %param.11) | copy-start | bytes 786436
  36.0 295.3 %all-gather.9.cloned.1.call-start = ((), (), s32[]{:S(2)}) async-start(), calls=%async_computation.1 | async-start | bytes 7962624 | tf_op jit(solution)/shard_map/all_gather | solution.py:250
  37.8 18.6 %collective-permute-start.1 = (bf16[4,1,8,128]{3,2,1,0:T(8,128)(2,1)S(1)}, bf16[4,1,8,128]{3,2,1,0:T(8,128)(2,1)S(1)}, u32[]{:S(2)}, u32[]{:S(2)}) collective-permute-start(bf16[4,1,8,128]{3,2,1,0:T(8,128)(2,1)S(1)} %get-tuple-element.221), channel_id=1, source_target_pairs={{4,0},{8,4},{12,8},{16,12},{20,16},{24,20},{28,24},{5,1},{9,5},{13... | collective-permute-start | bytes 24584 | tf_op jit(solution)/shard_map/ppermute | solution.py:40
  39.1 17.3 %collective-permute-start = (bf16[4,1,8,128]{3,2,1,0:T(8,128)(2,1)S(1)}, bf16[4,1,8,128]{3,2,1,0:T(8,128)(2,1)S(1)}, u32[]{:S(2)}, u32[]{:S(2)}) collective-permute-start(bf16[4,1,8,128]{3,2,1,0:T(8,128)(2,1)S(1)} %get-tuple-element.220), channel_id=1, source_target_pairs={{0,4},{4,8},{8,12},{12,16},{16,20},{20,24},{24,28},{1,5},{5,9},{9,... | collective-permute-start | bytes 24584 | tf_op jit(solution)/shard_map/ppermute | solution.py:38
  45.7 3.4 collective-permute-start.7
  49.2 7.9 %collective-permute-start.9 = (bf16[48,1,8,128]{3,0,1,2:T(8,128)(2,1)S(1)}, bf16[48,1,8,128]{3,0,1,2:T(8,128)(2,1)S(1)}, u32[]{:S(2)}, u32[]{:S(2)}) collective-permute-start(bf16[48,1,8,128]{3,0,1,2:T(8,128)(2,1)S(1)} %get-tuple-element.219), channel_id=1, source_target_pairs={{4,0},{8,4},{12,8},{16,12},{20,16},{24,20},{28,24},{5,1},{9,5},{13... | collective-permute-start | bytes 294920 | tf_op jit(solution)/shard_map/ppermute | solution.py:40
  50.5 8.1 %collective-permute-start.8 = (bf16[48,1,8,128]{3,0,1,2:T(8,128)(2,1)S(1)}, bf16[48,1,8,128]{3,0,1,2:T(8,128)(2,1)S(1)}, u32[]{:S(2)}, u32[]{:S(2)}) collective-permute-start(bf16[48,1,8,128]{3,0,1,2:T(8,128)(2,1)S(1)} %get-tuple-element.218), channel_id=1, source_target_pairs={{0,4},{4,8},{8,12},{12,16},{16,20},{20,24},{24,28},{1,5},{5,9},{9,... | collective-permute-start | bytes 294920 | tf_op jit(solution)/shard_map/ppermute | solution.py:38
  59.7 116.4 %collective-permute-start.10 = (bf16[16,4,8,128]{3,0,1,2:T(8,128)(2,1)S(1)}, bf16[16,4,8,128]{3,0,1,2:T(8,128)(2,1)S(1)}, u32[]{:S(2)}, u32[]{:S(2)}) collective-permute-start(bf16[16,4,8,128]{3,0,1,2:T(8,128)(2,1)S(1)} %copy.308), channel_id=1, source_target_pairs={{1,0},{2,1},{3,2},{5,4},{6,5},{7,6},{9,8},{10,9},{11,10},{13,12},{... | collective-permute-start | bytes 393224 | tf_op jit(solution)/shard_map/ppermute | solution.py:50
Sparse Core Ops, SparseCore 0:
  36.1 158.7 all-gather.6
  197.1 134.1 all-gather.8
